TPU v7x, 256 devices: a whole 4x4x8 slice. The times are simulated.
256 devices in a mesh: dp: 128 (over x, z, y_hi, core), shard: 2 (over y_lo).
Axes of the slice: x: 4, y: 4 (y_hi: 2, y_lo: 2; y = y_hi * 2 + y_lo), z: 8, core: 2. Of those that a mesh axis runs over, the one named last changes fastest.
Arguments:
- clips: bfloat16 [512, 5, 256, 512], P(('dp', 'shard')), may hold values from -16 to 16
- code_grad: bfloat16 [512, 5, 256, 18], P(('dp', 'shard')), may hold values from -6 to 6
- conv_weight: bfloat16 [1536, 512], replicated, may hold values from -0.15625 to 0.15625
- norm_gain: float32 [512], replicated, may hold values from 0.5 to 1.5
- proj_weight: bfloat16 [512, 18], replicated, may hold values from -0.25 to 0.25
- code_bias: float32 [18], replicated, may hold values from -1 to 1
- rotation: float32 [18, 18], replicated, may hold values from -1.5 to 1.5
- first_moment: float32 [1536, 512], P('shard'), may hold values from -4 to 4
- second_moment: float32 [1536, 512], P('shard'), may hold values from 0.01 to 0.3
Outputs:
- new_weight: bfloat16 [1536, 512], replicated
- first_moment_out: float32 [1536, 512], P('shard')
- second_moment_out: float32 [1536, 512], P('shard')
- input_grad: bfloat16 [512, 5, 256, 512], P(('dp', 'shard'))
- loss: float32 [], replicated
All inputs are finite; a program needn't handle non-finite values.
Results may differ from a plain program's by a relative error of at most 0.014.
Values may be sent and summed in bfloat16 or wider, within the bound.
No kernel may reach another device: no remote copies, remote signals or barrier semaphores. Data moves between devices by JAX's collectives and lax.ppermute only.
A program may use at most 128 MiB of HBM per device.

v0:
```python
import jax
import jax.numpy as jnp
from jax import lax
from jax.sharding import Mesh
from jax.sharding import PartitionSpec as P

DP = ("dp_0", "dp_1", "dp_2", "dp_3")
DP_SHARD = ("dp_0", "dp_1", "dp_2", "dp_3", "shard")


def one_axis_at_a_time(shard, axes):
    for axis in axes:
        shard = lax.psum(shard, axis)
    return shard


def split_up(shard, dim, count):
    before, after = (shard.shape[:dim], shard.shape[dim + 1 :])
    return jnp.moveaxis(shard.reshape(*before, count, -1, *after), dim, 0)


def sum_at_owner(shard, axis, dim):
    count = lax.axis_size(axis)
    tiles = lax.all_to_all(split_up(shard, dim, count), axis, 0, 0, tiled=True)
    return jnp.sum(tiles.astype(jnp.float32), axis=0)


def sum_at_owner_2(shard, axis, dim):
    count = lax.axis_size(axis)
    tiles = lax.all_to_all(split_up(shard, dim, count), axis, 0, 0, tiled=True)
    return jnp.sum(tiles, axis=0)


def sum_by_axis(shard, axes, dim):
    far, near = axes
    tiles = split_up(shard, dim, lax.axis_size(far))
    nearer = sum_at_owner_2(tiles, near, dim + 1)
    arrived = lax.all_to_all(nearer, far, split_axis=0, concat_axis=0, tiled=True)
    return arrived.sum(axis=0)


def filled_up(lines, count):
    spare = -len(lines) % count
    return jnp.pad(lines, [(0, spare)] + [(0, 0)] * (lines.ndim - 1))


def copy_for_each(shard, axis):
    copies = jnp.broadcast_to(shard, (lax.axis_size(axis), *shard.shape))
    return lax.all_to_all(copies, axis, split_axis=0, concat_axis=0, tiled=True)


def joined_along(tiles, dim):
    shape = list(tiles.shape[1:])
    shape[dim] *= tiles.shape[0]
    return jnp.moveaxis(tiles, 0, dim).reshape(shape)


def gathered_by_axis(shard, axes, dim):
    far, near = axes
    tiles = copy_for_each(copy_for_each(shard, far), near)
    return joined_along(tiles.swapaxes(0, 1).reshape(-1, *shard.shape), dim)


def total_of(shard, axes):
    lines = shard.reshape(-1, shard.shape[-1])
    own = sum_by_axis(filled_up(lines, lax.axis_size(axes[0]) * lax.axis_size(axes[1])), axes, 0)
    whole = gathered_by_axis(own, axes, 0)
    return whole[: len(lines)].reshape(shard.shape)


def collect(shard, axis, dim):
    tiles = copy_for_each(shard, axis)
    return joined_along(tiles, dim)


def stacked_taps(block):
    batch, frames, sites, width = block.shape
    padded = jnp.pad(block, ((0, 0), (2, 0), (0, 0), (0, 0)))
    taps = [padded[:, 2 - k : 2 - k + frames] for k in range(3)]
    return jnp.concatenate(taps, axis=3).reshape(batch * frames * sites, 3 * width)


def forward(block, conv_weight, norm_gain, proj_weight, code_bias, rotation):
    width = block.shape[3]
    stacked = stacked_taps(block)
    hidden = block.reshape(-1, width).astype(jnp.float32) + jnp.dot(
        stacked, conv_weight, preferred_element_type=jnp.float32
    )
    inverse = lax.rsqrt(jnp.mean(hidden * hidden, axis=1, keepdims=True) + 1e-06)
    unit = hidden * inverse
    normed = (unit * norm_gain).astype(jnp.bfloat16)
    latent = jnp.dot(normed, proj_weight, preferred_element_type=jnp.float32) + code_bias
    rotated = jnp.dot(latent, rotation, precision=lax.Precision.HIGHEST)
    codes = jnp.tanh(rotated)
    return (stacked, inverse, unit, rotated, codes)


def token_terms(rotated, codes, cotangent):
    probs = (1.0 + codes) / 2.0
    logit = 2.0 * rotated
    entropy = jax.nn.softplus(logit) - logit * probs
    token_loss = cotangent * codes + 0.25 * (rotated - codes) ** 2 + 0.1 * entropy
    return (probs, logit, jnp.sum(token_loss))


def backward(
    block, cotangent, conv_weight, norm_gain, proj_weight, rotation, saved, lean, clip_count
):
    stacked, inverse, unit, rotated, codes = saved
    probs = (1.0 + codes) / 2.0
    logit = 2.0 * rotated
    slope = 1.0 - codes * codes
    d_rot = (
        cotangent * slope
        + 0.5 * (rotated - codes) * (1.0 - slope)
        - 0.2 * logit * probs * (1.0 - probs)
        - 0.05 * slope * lean
    ) / clip_count
    d_lat = jnp.dot(d_rot, rotation.T, precision=lax.Precision.HIGHEST)
    d_norm = jnp.dot(d_lat, proj_weight.astype(jnp.float32).T, precision=lax.Precision.HIGHEST)
    scaled = d_norm * norm_gain
    d_hidden = inverse * (scaled - unit * jnp.mean(scaled * unit, axis=1, keepdims=True))
    d_conv = d_hidden.astype(jnp.bfloat16)
    batch, frames, sites, width = block.shape
    d_taps = lax.dot_general(
        d_conv, conv_weight, (((1,), (1,)), ((), ())), preferred_element_type=jnp.float32
    )
    d_taps = d_taps.reshape(batch, frames, sites, 3, width)
    padded = jnp.pad(d_taps, ((0, 0), (0, 2), (0, 0), (0, 0), (0, 0)))
    back = (
        padded[:, 0:frames, :, 0, :]
        + padded[:, 1 : frames + 1, :, 1, :]
        + padded[:, 2 : frames + 2, :, 2, :]
    )
    input_grad = (d_hidden.reshape(batch, frames, sites, width) + back).astype(jnp.bfloat16)
    return (stacked, d_conv, input_grad)


def on_device(
    clips,
    code_grad,
    conv_weight,
    norm_gain,
    proj_weight,
    code_bias,
    rotation,
    first_moment,
    second_moment,
):
    bit_count = code_grad.shape[3]
    devices = lax.axis_size(DP) * lax.axis_size("shard")
    clip_count = clips.shape[0] * devices
    token_count = clips.shape[0] * clips.shape[1] * clips.shape[2] * devices
    cotangent = code_grad.reshape(-1, bit_count).astype(jnp.float32)
    saved = forward(clips, conv_weight, norm_gain, proj_weight, code_bias, rotation)
    probs, logit, loss_part = token_terms(saved[3], saved[4], cotangent)
    bit_total, loss_total = (
        one_axis_at_a_time(jnp.sum(probs, axis=0), DP_SHARD),
        one_axis_at_a_time(loss_part, DP_SHARD),
    )
    bit_mean = bit_total / token_count
    code_entropy = jnp.sum(
        -bit_mean * jnp.log(bit_mean) - (1.0 - bit_mean) * jnp.log(1.0 - bit_mean)
    )
    loss = loss_total / token_count - 0.1 * code_entropy
    lean = jnp.log((1.0 - bit_mean) / bit_mean)
    stacked, d_conv, input_grad = backward(
        clips, cotangent, conv_weight, norm_gain, proj_weight, rotation, saved, lean, clip_count
    )
    owned_rows = first_moment.shape[0]
    group_part = sum_at_owner(
        lax.dot_general(
            stacked, d_conv, (((0,), (0,)), ((), ())), preferred_element_type=jnp.float32
        ).astype(jnp.bfloat16),
        "shard",
        0,
    )
    grad_owned = total_of(group_part, (("dp_0", "dp_1", "dp_2"), "dp_3"))
    first_out = 0.9 * first_moment + 0.1 * grad_owned
    second_out = 0.99 * second_moment + 0.01 * grad_owned * grad_owned
    owner = lax.axis_index("shard")
    own_weight = lax.dynamic_slice_in_dim(conv_weight, owner * owned_rows, owned_rows, 0).astype(
        jnp.float32
    )
    stepped = (own_weight - 0.001 * first_out / (jnp.sqrt(second_out) + 1e-08)).astype(jnp.bfloat16)
    new_weight = collect(stepped, "shard", 0)
    return (new_weight, first_out, second_out, input_grad, loss)


def solution(mesh):
    finer = Mesh(
        mesh.devices.reshape(4, 8, 2, 2, mesh.shape["shard"]),
        ("dp_0", "dp_1", "dp_2", "dp_3", "shard"),
    )
    in_specs = (
        P(DP_SHARD, None, None, None),
        P(DP_SHARD, None, None, None),
        P(),
        P(),
        P(),
        P(),
        P(),
        P("shard", None),
        P("shard", None),
    )
    out_specs = (P(), P("shard", None), P("shard", None), P(DP_SHARD, None, None, None), P())
    return jax.shard_map(
        on_device, mesh=finer, in_specs=in_specs, out_specs=out_specs, check_vma=False
    )
```

profile of v0, /device:TPU:1, one launch (start us, length us, event | category | flops | bytes accessed | tf_op | source)
XLA Modules:
  0.0 238.2 jit_solution(2002389347079798934)
XLA Ops:
  1.7 2.7 %pad_slice_fusion.3 = (bf16[2,5,256,512]{3,2,1,0:T(8,128)(2,1)S(1)}, bf16[2,5,256,512]{3,2,1,0:T(8,128)(2,1)S(1)}) fusion(bf16[2,5,256,512]{3,2,1,0:T(8,128)(2,1)} %param.9), kind=kLoop, calls=%fused_computation.14 | loop fusion | bytes 7864320 | tf_op jit(solution)/shard_map/slice | solution.py:79
  5.9 4.6 %multiply_reduce_fusion.1 = (f32[2560]{0:T(1024)S(1)}, f32[2560,512]{1,0:T(8,128)S(1)}) fusion(bf16[2560,1536]{1,0:T(8,128)(2,1)S(1)} %bitcast.29, bf16[1536,512]{1,0:T(8,128)(2,1)S(1)} %copy-done.6, bf16[2560,512]{1,0:T(8,128)(2,1)S(1)} %bitcast.27), kind=kOutput, calls=%fused_computation.11 | convolution fusion | flops 4031772160 | bytes 17311744 | tf_op jit(solution)/shard_map/dot_general | solution.py:86
  14.1 9.9 %all-reduce.3 = (f32[18]{0:T(128)S(1)}, f32[]{:T(128)}) all-reduce(f32[18]{0:T(128)S(1)} %get-tuple-element.6, f32[]{:T(128)} %get-tuple-element.5), channel_id=1, replica_groups=mesh['dp_0'=4,'dp_1'=8,'dp_2'=2,'dp_3'=2,'shard'=2] {'dp_0'}, use_global_device_ids=true, to_apply=%region_2.3 | all-reduce | flops 19 | bytes 152 | tf_op jit(solution)/shard_map/psum | solution.py:13
  24.0 16.9 %all-reduce.2 = (f32[18]{0:T(128)S(1)}, f32[]{:T(128)}) all-reduce(f32[18]{0:T(128)S(1)} %get-tuple-element.9, f32[]{:T(128)} %get-tuple-element.10), channel_id=1, replica_groups=mesh['dp_0'=4,'dp_1'=8,'dp_2'=2,'dp_3'=2,'shard'=2] {'dp_1'}, use_global_device_ids=true, to_apply=%region_3.4 | all-reduce | flops 19 | bytes 152 | tf_op jit(solution)/shard_map/psum | solution.py:13
  40.9 5.9 %all-reduce.6 = (f32[18]{0:T(128)S(1)}, f32[]{:T(128)}) all-reduce(f32[18]{0:T(128)S(1)} %get-tuple-element.7, f32[]{:T(128)} %get-tuple-element.8), channel_id=1, replica_groups=mesh['dp_0'=4,'dp_1'=8,'dp_2'=2,'dp_3'=2,'shard'=2] {'dp_2'}, use_global_device_ids=true, to_apply=%region_4.5 | all-reduce | flops 19 | bytes 152 | tf_op jit(solution)/shard_map/psum | solution.py:13
  46.8 10.3 %all-reduce.5 = (f32[18]{0:T(128)S(1)}, f32[]{:T(128)}) all-reduce(f32[18]{0:T(128)S(1)} %get-tuple-element.15, f32[]{:T(128)} %get-tuple-element.16), channel_id=1, replica_groups=mesh['dp_0'=4,'dp_1'=8,'dp_2'=2,'dp_3'=2,'shard'=2] {'dp_3'}, use_global_device_ids=true, to_apply=%region_5.6 | all-reduce | flops 19 | bytes 152 | tf_op jit(solution)/shard_map/psum | solution.py:13
  57.1 4.6 %all-reduce.4 = (f32[18]{0:T(128)S(1)}, f32[]{:T(128)}) all-reduce(f32[18]{0:T(128)S(1)} %get-tuple-element.13, f32[]{:T(128)} %get-tuple-element.14), channel_id=1, replica_groups=mesh['dp_0'=4,'dp_1'=8,'dp_2'=2,'dp_3'=2,'shard'=2] {'shard'}, use_global_device_ids=true, to_apply=%region_6.7 | all-reduce | flops 19 | bytes 152 | tf_op jit(solution)/shard_map/psum | solution.py:13
  62.9 5.8 %multiply_reduce_fusion = (f32[2560]{0:T(1024)S(1)}, f32[2560,512]{1,0:T(8,128)S(1)}) fusion(f32[2560,512]{1,0:T(8,128)} %copy-done.3, f32[2560]{0:T(1024)S(1)} %add_rsqrt_fusion, f32[512]{0:T(512)S(1)} %copy-done.8, f32[2560,18]{0,1:T(8,128)S(1)} %fusion.20, bf16[512,18]{0,1:T(8,128)(2,1)S(1)} %copy-done), kind=kOutput, calls=%fused_computation.9 | convolution fusion | flops 288355840 | bytes 10711040 | tf_op jit(solution)/shard_map/dot_general | solution.py:120
  68.7 1.6 subtract_multiply_fusion
  70.8 4.3 %convolution_convert_fusion = bf16[1536,512]{1,0:T(8,128)(2,1)S(1)} fusion(bf16[2560,1536]{1,0:T(8,128)(2,1)S(1)} %bitcast.32, f32[2560,512]{1,0:T(8,128)S(1)} %subtract_multiply_fusion), kind=kOutput, calls=%fused_computation.17 | convolution fusion | flops 4028628992 | bytes 14680064 | tf_op jit(solution)/shard_map/dot_general | solution.py:172
  75.1 20.2 %all_to_all.30 = bf16[2,768,512]{2,1,0:T(8,128)(2,1)S(1)} all-to-all(bf16[2,768,512]{2,1,0:T(8,128)(2,1)S(1)} %bitcast.35), channel_id=1, replica_groups=mesh['dp_0'=4,'dp_1'=8,'dp_2'=2,'dp_3'=2,'shard'=2] {'shard'}, dimensions={0} | all-to-all | bytes 3145728 | tf_op jit(solution)/shard_map/all_to_all | solution.py:24
  95.2 1.5 convert_reduce_fusion
  96.7 1.5 reshape_reshape.6
  99.1 7.1 %all_to_all.31 = f32[2,64,6,512]{3,1,2,0:T(8,128)S(1)} all-to-all(f32[2,64,6,512]{3,1,2,0:T(8,128)S(1)} %copy.26), channel_id=1, replica_groups=mesh['dp_0'=4,'dp_1'=8,'dp_2'=2,'dp_3'=2,'shard'=2] {'dp_3'}, dimensions={0} | all-to-all | bytes 3145728 | tf_op jit(solution)/shard_map/all_to_all | solution.py:30
  106.9 36.2 %all_to_all.32 = f32[64,6,512]{2,1,0:T(8,128)S(1)} all-to-all(f32[64,6,512]{2,1,0:T(8,128)S(1)} %copy.27), channel_id=1, replica_groups=mesh['dp_0'=4,'dp_1'=8,'dp_2'=2,'dp_3'=2,'shard'=2] {'dp_0','dp_1','dp_2'}, dimensions={0} | all-to-all | bytes 1572864 | tf_op jit(solution)/shard_map/all_to_all | solution.py:38
  144.3 6.9 %all-to-all-start.3 = ((f32[64,6,512]{2,1,0:T(8,128)}), f32[64,6,512]{2,1,0:T(8,128)S(1)}, u32[]{:S(2)}, u32[]{:S(2)}) async-start(f32[64,6,512]{2,1,0:T(8,128)} %broadcast_in_dim.6), calls=%async_computation.3 | async-start | bytes 2097152 | tf_op jit(solution)/shard_map/all_to_all | solution.py:49
  151.3 10.3 %fusion.6 = f32[2560,1536]{1,0:T(8,128)} fusion(bf16[1536,512]{1,0:T(8,128)(2,1)S(1)} %copy-done.7, f32[2560,512]{1,0:T(8,128)} %copy-done.2), kind=kOutput, calls=%fused_computation.24 | convolution fusion | flops 4027842560 | bytes 22544384 | tf_op jit(solution)/shard_map/dot_general | solution.py:125
  161.5 26.1 %reshape.52 = f32[2,5,256,3,512]{4,3,2,1,0:T(4,128)} reshape(f32[2560,1536]{1,0:T(8,128)} %fusion.6) | data formatting | bytes 31457280 | tf_op jit(solution)/shard_map/reshape | solution.py:128
  188.3 6.0 %all_to_all.33 = f32[2,64,6,512]{3,1,2,0:T(8,128)S(1)} all-to-all(f32[2,64,6,512]{3,1,2,0:T(8,128)S(1)} %broadcast_in_dim.7), channel_id=1, replica_groups=mesh['dp_0'=4,'dp_1'=8,'dp_2'=2,'dp_3'=2,'shard'=2] {'dp_3'}, dimensions={0} | all-to-all | bytes 3145728 | tf_op jit(solution)/shard_map/all_to_all | solution.py:49
  195.2 1.4 reshape_reshape.7
  196.6 5.3 %subtract_convert_fusion = (bf16[768,512]{1,0:T(8,128)(2,1)S(1)}, f32[768,512]{1,0:T(8,128)}, f32[768,512]{1,0:T(8,128)}) fusion(bf16[1536,512]{1,0:T(8,128)(2,1)} %param.11, s32[]{:T(128)S(6)} %select_n.7, f32[768,512]{1,0:T(8,128)} %reshape_reshape.7, f32[768,512]{1,0:T(8,128)} %param.16, f32[768,512]{1,0:T(8,128)} %param.17), kind=kLoop, calls=%fused_computation.22 | loop fusion | flops 5111808 | bytes 9437188 | tf_op jit(solution)/shard_map/convert_element_type | solution.py:185
  203.1 3.7 %all-to-all-start.5 = ((bf16[2,768,512]{2,1,0:T(8,128)(2,1)}), bf16[2,768,512]{2,1,0:T(8,128)(2,1)S(1)}, u32[]{:S(2)}, u32[]{:S(2)}) async-start(bf16[2,768,512]{2,1,0:T(8,128)(2,1)} %broadcast_in_dim.8), calls=%async_computation.5 | async-start | bytes 3145728 | tf_op jit(solution)/shard_map/all_to_all | solution.py:49
  206.8 21.4 %fusion.1 = f32[2,5,256,1,512]{4,3,2,1,0:T(1,128)} fusion(f32[2,5,256,3,512]{4,3,2,1,0:T(4,128)} %reshape.52), kind=kLoop, calls=%fused_computation.4 | loop fusion | flops 2621440 | bytes 31457280 | tf_op jit(solution)/shard_map/add | solution.py:131
  229.5 6.5 %fusion.2 = bf16[2,5,256,512]{3,2,1,0:T(8,128)(2,1)} fusion(f32[2,5,256,512]{3,2,1,0:T(8,128)} %bitcast.24, f32[2,5,256,1,512]{4,3,2,1,0:T(1,128)} %fusion.1), kind=kLoop, calls=%fused_computation.6 | loop fusion | flops 2621440 | bytes 13107200 | tf_op jit(solution)/shard_map/convert_element_type | solution.py:135
  (53 shorter events, 14.5 us)
Async XLA Ops:
  0.6 10.0 %copy-start = (bf16[512,18]{0,1:T(8,128)(2,1)S(1)}, bf16[512,18]{0,1:T(8,128)(2,1)}, u32[]{:S(2)}) copy-start(bf16[512,18]{0,1:T(8,128)(2,1)} %param.13) | copy-start | bytes 55300
  1.6 2.8 %copy-start.4 = (bf16[2,5,256,512]{3,2,1,0:T(8,128)(2,1)S(1)}, bf16[2,5,256,512]{3,2,1,0:T(8,128)(2,1)}, u32[]{:S(2)}) copy-start(bf16[2,5,256,512]{3,2,1,0:T(8,128)(2,1)} %param.9) | copy-start | bytes 7864324
  4.5 1.4 copy-start.6
  5.4 5.2 %copy-start.5 = (bf16[2,5,256,1536]{3,2,1,0:T(8,128)(2,1)}, bf16[2,5,256,1536]{3,2,1,0:T(8,128)(2,1)S(1)}, u32[]{:S(2)}) copy-start(bf16[2,5,256,1536]{3,2,1,0:T(8,128)(2,1)S(1)} %pad_maximum_fusion) | copy-start | bytes 23592964
  5.9 4.7 %copy-start.8 = (f32[512]{0:T(512)S(1)}, f32[512]{0:T(512)}, u32[]{:S(2)}) copy-start(f32[512]{0:T(512)} %param.12) | copy-start | bytes 6148
  5.9 4.7 %copy-start.9 = (f32[18]{0:T(128)S(1)}, f32[18]{0:T(128)}, u32[]{:S(2)}) copy-start(f32[18]{0:T(128)} %param.14) | copy-start | bytes 220
  10.6 2.3 copy-start.3
  10.6 2.3 copy-start.10
  62.3 6.4 %slice-start = ((s8[5242880]{0:T(1024)(128)(4,1)}), s8[4194304]{0:T(1024)(128)(4,1)S(1)}, s32[]{:S(2)}) async-start(s8[5242880]{0:T(1024)(128)(4,1)} %bitcast.25), calls=%async_computation.6 | async-start | bytes 8388608
  62.8 5.9 %slice-start.1 = ((s8[5242880]{0:T(1024)(128)(4,1)}), s8[1048576]{0:T(1024)(128)(4,1)S(1)}, s32[]{:S(2)}) async-start(s8[5242880]{0:T(1024)(128)(4,1)} %bitcast.25), calls=%async_computation.7 | async-start | bytes 2097152
  62.9 7.5 %slice-start.2 = ((s8[7864320]{0:T(1024)(128)(4,1)}), s8[4194304]{0:T(1024)(128)(4,1)S(1)}, s32[]{:S(2)}) async-start(s8[7864320]{0:T(1024)(128)(4,1)} %bitcast.30), calls=%async_computation.8 | async-start | bytes 8388608
  68.7 2.0 slice-start.3
  70.8 4.3 %copy-start.2 = (f32[2560,512]{1,0:T(8,128)}, f32[2560,512]{1,0:T(8,128)S(1)}, u32[]{:S(2)}) copy-start(f32[2560,512]{1,0:T(8,128)S(1)} %subtract_multiply_fusion) | copy-start | bytes 15728644
  143.1 8.1 %copy-start.7 = (bf16[1536,512]{1,0:T(8,128)(2,1)S(1)}, bf16[1536,512]{1,0:T(8,128)(2,1)}, u32[]{:S(2)}) copy-start(bf16[1536,512]{1,0:T(8,128)(2,1)} %param.11) | copy-start | bytes 4718596
  144.3 43.3 %all-to-all-start.3 = ((f32[64,6,512]{2,1,0:T(8,128)}), f32[64,6,512]{2,1,0:T(8,128)S(1)}, u32[]{:S(2)}, u32[]{:S(2)}) async-start(f32[64,6,512]{2,1,0:T(8,128)} %broadcast_in_dim.6), calls=%async_computation.3 | async-start | bytes 2097152 | tf_op jit(solution)/shard_map/all_to_all | solution.py:49
  203.1 32.8 %all-to-all-start.5 = ((bf16[2,768,512]{2,1,0:T(8,128)(2,1)}), bf16[2,768,512]{2,1,0:T(8,128)(2,1)S(1)}, u32[]{:S(2)}, u32[]{:S(2)}) async-start(bf16[2,768,512]{2,1,0:T(8,128)(2,1)} %broadcast_in_dim.8), calls=%async_computation.5 | async-start | bytes 3145728 | tf_op jit(solution)/shard_map/all_to_all | solution.py:49
  229.5 7.6 %copy-start.1 = (bf16[512,18]{0,1:T(8,128)(2,1)S(1)}, bf16[512,18]{0,1:T(8,128)(2,1)}, u32[]{:S(2)}) copy-start(bf16[512,18]{0,1:T(8,128)(2,1)} %param.13) | copy-start | bytes 55300
where the time goes:
time: 240 us; the launch traced here: 238 us
  blocking collectives  117 us (49%)
  local copies, waits for them, and re-layouts  41.5 us (17%)
  other arithmetic  38 us (16%)
  matrix products  27.8 us (12%)
  starting transfers between devices  10.6 us (4%)
  between operations  3.36 us (1%)
    psum x5, blocking collectives, one_axis_at_a_time(): shard = lax.psum(shard, axis)  47.5 us
    all_to_all x1, blocking collectives, sum_by_axis(): lax.all_to_all(nearer, far, split_axis=0, concat_axis=0, tiled=True)  36.2 us
    reshape x1, local copies, waits for them, and re-layouts, backward(): d_taps = d_taps.reshape(batch, frames, sites, 3, width)  26.1 us
    add x1, other arithmetic, backward(): padded[:, 0:frames, :, 0, :] + padded[:, 1:frames + 1, :, 1, :]  21.4 us
    all_to_all x1, blocking collectives, sum_at_owner(): tiles = lax.all_to_all(split_up(shard, dim, count), axis, 0, 0, tiled=True)  20.2 us
    all_to_all x2, starting transfers between devices, copy_for_each(): return lax.all_to_all(copies, axis, split_axis=0, concat_axis=0, tiled=True)  10.6 us
    dot_general x1, matrix products, backward(): lax.dot_general(d_conv, conv_weight, (((1,), (1,)), ((), ())), preferred_...  10.3 us
    all_to_all x1, blocking collectives, sum_at_owner_2(): tiles = lax.all_to_all(split_up(shard, dim, count), axis, 0, 0, tiled=True)  7.14 us
  transfers between devices with their start and end apart: 2, of which 0 were waited for; matrix products, arithmetic and copies ran while one was open for 27% of the time, Pallas kernels for 0%

commit v1 on v0

--- a/solution.py
+++ b/solution.py
@@ -10,7 +10,8 @@
 
 def one_axis_at_a_time(shard, axes):
     for axis in axes:
-        shard = lax.psum(shard, axis)
+        blocks = lax.all_gather(shard, axis, axis=0, tiled=False)
+        shard = blocks.sum(axis=0)
     return shard
 
 

time: 240 us -> 258 us (1.075)
  local copies, waits for them, and re-layouts: 41.5 us -> 56.4 us
  between operations: 3.36 us -> 6.62 us
  other arithmetic: 38 us -> 41.1 us
  blocking collectives: 117 us -> 114 us
    psum x5 -> x0, blocking collectives: 47.5 us -> none  [one_axis_at_a_time(): shard = lax.psum(shard, axis)]
    unnamed x0 -> x5, blocking collectives: none -> 44.4 us
    unnamed x31 -> x56, local copies, waits for them, and re-layouts: 3.59 us -> 18 us
    reduce_sum x0 -> x10, other arithmetic: none -> 3.11 us  [one_axis_at_a_time(): shard = blocks.sum(axis=0)]
  transfers between devices with their start and end apart: 2 -> 2, of which waited for: 0 -> 0; matrix products, arithmetic and copies ran while one was open for 27% -> 25% of each run, Pallas kernels for 0% -> 0%
where the time goes in v1:
time: 258 us; the launch traced here: 256 us
  blocking collectives  114 us (44%)
  local copies, waits for them, and re-layouts  56.4 us (22%)
  other arithmetic  41.1 us (16%)
  matrix products  27.8 us (11%)
  starting transfers between devices  10.6 us (4%)
  between operations  6.62 us (3%)
    unnamed x5, blocking collectives  44.4 us
    all_to_all x1, blocking collectives, sum_by_axis(): lax.all_to_all(nearer, far, split_axis=0, concat_axis=0, tiled=True)  36.2 us
    reshape x1, local copies, waits for them, and re-layouts, backward(): d_taps = d_taps.reshape(batch, frames, sites, 3, width)  26.1 us
    add x1, other arithmetic, backward(): padded[:, 0:frames, :, 0, :] + padded[:, 1:frames + 1, :, 1, :]  21.4 us
    all_to_all x1, blocking collectives, sum_at_owner(): tiles = lax.all_to_all(split_up(shard, dim, count), axis, 0, 0, tiled=True)  20.2 us
    unnamed x56, local copies, waits for them, and re-layouts  18 us
    all_to_all x2, starting transfers between devices, copy_for_each(): return lax.all_to_all(copies, axis, split_axis=0, concat_axis=0, tiled=True)  10.6 us
    dot_general x1, matrix products, backward(): lax.dot_general(d_conv, conv_weight, (((1,), (1,)), ((), ())), preferred_...  10.3 us
  transfers between devices with their start and end apart: 2, of which 0 were waited for; matrix products, arithmetic and copies ran while one was open for 25% of the time, Pallas kernels for 0%

profile of v1, /device:TPU:1, one launch (start us, length us, event | category | flops | bytes accessed | tf_op | source)
XLA Modules:
  0.0 256.3 jit_solution(8834123953920573864)
XLA Ops:
  11.3 2.7 %pad_slice_fusion.3 = (bf16[2,5,256,512]{3,2,1,0:T(8,128)(2,1)S(1)}, bf16[2,5,256,512]{3,2,1,0:T(8,128)(2,1)S(1)}) fusion(bf16[2,5,256,512]{3,2,1,0:T(8,128)(2,1)} %param.9), kind=kLoop, calls=%fused_computation.14 | loop fusion | bytes 7864320 | tf_op jit(solution)/shard_map/slice | solution.py:80
  15.6 4.6 %multiply_reduce_fusion.1 = (f32[2560]{0:T(1024)S(1)}, f32[2560,512]{1,0:T(8,128)S(1)}) fusion(bf16[2560,1536]{1,0:T(8,128)(2,1)S(1)} %bitcast.44, bf16[1536,512]{1,0:T(8,128)(2,1)S(1)} %copy-done.6, bf16[2560,512]{1,0:T(8,128)(2,1)S(1)} %bitcast.42), kind=kOutput, calls=%fused_computation.11 | convolution fusion | flops 4031772160 | bytes 17311744 | tf_op jit(solution)/shard_map/dot_general | solution.py:87
  25.4 9.3 %all-reduce.13 = (f32[72]{0:T(128)S(1)}, f32[4]{0:T(128)S(1)}) all-reduce(f32[72]{0:T(128)S(1)} %dynamic-update-slice, f32[4]{0:T(128)S(1)} %dynamic-update-slice.5), channel_id=2, replica_groups=mesh['dp_0'=4,'dp_1'=8,'dp_2'=2,'dp_3'=2,'shard'=2] {'dp_0'}, use_global_device_ids=true, to_apply=%add.2 | all-reduce | flops 76 | bytes 608
  37.0 16.2 %all-reduce.12 = (f32[144]{0:T(256)S(1)}, f32[8]{0:T(128)S(1)}) all-reduce(f32[144]{0:T(256)S(1)} %dynamic-update-slice.1, f32[8]{0:T(128)S(1)} %dynamic-update-slice.6), channel_id=3, replica_groups=mesh['dp_0'=4,'dp_1'=8,'dp_2'=2,'dp_3'=2,'shard'=2] {'dp_1'}, use_global_device_ids=true, to_apply=%add.3 | all-reduce | flops 152 | bytes 1216
  53.9 1.4 dynamic-update-slice.7
  55.6 5.3 %all-reduce.16 = (f32[36]{0:T(128)S(1)}, f32[2]{0:T(128)S(1)}) all-reduce(f32[36]{0:T(128)S(1)} %dynamic-update-slice.2, f32[2]{0:T(128)S(1)} %dynamic-update-slice.7), channel_id=4, replica_groups=mesh['dp_0'=4,'dp_1'=8,'dp_2'=2,'dp_3'=2,'shard'=2] {'dp_2'}, use_global_device_ids=true, to_apply=%add.4 | all-reduce | flops 38 | bytes 304
  63.1 9.7 %all-reduce.15 = (f32[36]{0:T(128)S(1)}, f32[2]{0:T(128)S(1)}) all-reduce(f32[36]{0:T(128)S(1)} %dynamic-update-slice.3, f32[2]{0:T(128)S(1)} %dynamic-update-slice.8), channel_id=5, replica_groups=mesh['dp_0'=4,'dp_1'=8,'dp_2'=2,'dp_3'=2,'shard'=2] {'dp_3'}, use_global_device_ids=true, to_apply=%add.5 | all-reduce | flops 38 | bytes 304
  75.1 3.9 %all-reduce.14 = (f32[36]{0:T(128)S(1)}, f32[2]{0:T(128)S(1)}) all-reduce(f32[36]{0:T(128)S(1)} %dynamic-update-slice.4, f32[2]{0:T(128)S(1)} %dynamic-update-slice.9), channel_id=6, replica_groups=mesh['dp_0'=4,'dp_1'=8,'dp_2'=2,'dp_3'=2,'shard'=2] {'shard'}, use_global_device_ids=true, to_apply=%add.6 | all-reduce | flops 38 | bytes 304
  80.3 5.8 %multiply_reduce_fusion = (f32[2560]{0:T(1024)S(1)}, f32[2560,512]{1,0:T(8,128)S(1)}) fusion(f32[2560,512]{1,0:T(8,128)} %copy-done.3, f32[2560]{0:T(1024)S(1)} %add_rsqrt_fusion, f32[512]{0:T(512)S(1)} %copy-done.8, f32[2560,18]{0,1:T(8,128)S(1)} %fusion.20, bf16[512,18]{0,1:T(8,128)(2,1)S(1)} %copy-done), kind=kOutput, calls=%fused_computation.9 | convolution fusion | flops 288355840 | bytes 10711040 | tf_op jit(solution)/shard_map/dot_general | solution.py:121
  86.2 1.6 subtract_multiply_fusion
  88.2 4.3 %convolution_convert_fusion = bf16[1536,512]{1,0:T(8,128)(2,1)S(1)} fusion(bf16[2560,1536]{1,0:T(8,128)(2,1)S(1)} %bitcast.47, f32[2560,512]{1,0:T(8,128)S(1)} %subtract_multiply_fusion), kind=kOutput, calls=%fused_computation.17 | convolution fusion | flops 4028628992 | bytes 14680064 | tf_op jit(solution)/shard_map/dot_general | solution.py:173
  92.5 20.2 %all_to_all.32 = bf16[2,768,512]{2,1,0:T(8,128)(2,1)S(1)} all-to-all(bf16[2,768,512]{2,1,0:T(8,128)(2,1)S(1)} %bitcast.50), channel_id=1, replica_groups=mesh['dp_0'=4,'dp_1'=8,'dp_2'=2,'dp_3'=2,'shard'=2] {'shard'}, dimensions={0} | all-to-all | bytes 3145728 | tf_op jit(solution)/shard_map/all_to_all | solution.py:25
  112.7 1.5 convert_reduce_fusion
  114.2 1.5 reshape_reshape.6
  116.6 7.1 %all_to_all.30 = f32[2,64,6,512]{3,1,2,0:T(8,128)S(1)} all-to-all(f32[2,64,6,512]{3,1,2,0:T(8,128)S(1)} %copy.31), channel_id=1, replica_groups=mesh['dp_0'=4,'dp_1'=8,'dp_2'=2,'dp_3'=2,'shard'=2] {'dp_3'}, dimensions={0} | all-to-all | bytes 3145728 | tf_op jit(solution)/shard_map/all_to_all | solution.py:31
  124.4 36.2 %all_to_all.33 = f32[64,6,512]{2,1,0:T(8,128)S(1)} all-to-all(f32[64,6,512]{2,1,0:T(8,128)S(1)} %copy.32), channel_id=1, replica_groups=mesh['dp_0'=4,'dp_1'=8,'dp_2'=2,'dp_3'=2,'shard'=2] {'dp_0','dp_1','dp_2'}, dimensions={0} | all-to-all | bytes 1572864 | tf_op jit(solution)/shard_map/all_to_all | solution.py:39
  161.8 6.9 %all-to-all-start.3 = ((f32[64,6,512]{2,1,0:T(8,128)}), f32[64,6,512]{2,1,0:T(8,128)S(1)}, u32[]{:S(2)}, u32[]{:S(2)}) async-start(f32[64,6,512]{2,1,0:T(8,128)} %broadcast_in_dim.6), calls=%async_computation.3 | async-start | bytes 2097152 | tf_op jit(solution)/shard_map/all_to_all | solution.py:50
  168.7 10.3 %fusion.6 = f32[2560,1536]{1,0:T(8,128)} fusion(bf16[1536,512]{1,0:T(8,128)(2,1)S(1)} %copy-done.7, f32[2560,512]{1,0:T(8,128)} %copy-done.2), kind=kOutput, calls=%fused_computation.24 | convolution fusion | flops 4027842560 | bytes 22544384 | tf_op jit(solution)/shard_map/dot_general | solution.py:126
  179.0 26.1 %reshape.57 = f32[2,5,256,3,512]{4,3,2,1,0:T(4,128)} reshape(f32[2560,1536]{1,0:T(8,128)} %fusion.6) | data formatting | bytes 31457280 | tf_op jit(solution)/shard_map/reshape | solution.py:129
  205.7 6.0 %all_to_all.31 = f32[2,64,6,512]{3,1,2,0:T(8,128)S(1)} all-to-all(f32[2,64,6,512]{3,1,2,0:T(8,128)S(1)} %broadcast_in_dim.7), channel_id=1, replica_groups=mesh['dp_0'=4,'dp_1'=8,'dp_2'=2,'dp_3'=2,'shard'=2] {'dp_3'}, dimensions={0} | all-to-all | bytes 3145728 | tf_op jit(solution)/shard_map/all_to_all | solution.py:50
  214.0 5.3 %subtract_convert_fusion = (bf16[768,512]{1,0:T(8,128)(2,1)S(1)}, f32[768,512]{1,0:T(8,128)}, f32[768,512]{1,0:T(8,128)}) fusion(bf16[1536,512]{1,0:T(8,128)(2,1)} %param.11, s32[]{:T(128)S(6)} %select_n.7, f32[768,512]{1,0:T(8,128)} %reshape_reshape.7, f32[768,512]{1,0:T(8,128)} %param.16, f32[768,512]{1,0:T(8,128)} %param.17), kind=kLoop, calls=%fused_computation.22 | loop fusion | flops 5111808 | bytes 9437188 | tf_op jit(solution)/shard_map/convert_element_type | solution.py:186
  220.6 3.7 %all-to-all-start.5 = ((bf16[2,768,512]{2,1,0:T(8,128)(2,1)}), bf16[2,768,512]{2,1,0:T(8,128)(2,1)S(1)}, u32[]{:S(2)}, u32[]{:S(2)}) async-start(bf16[2,768,512]{2,1,0:T(8,128)(2,1)} %broadcast_in_dim.8), calls=%async_computation.5 | async-start | bytes 3145728 | tf_op jit(solution)/shard_map/all_to_all | solution.py:50
  224.2 21.4 %fusion.1 = f32[2,5,256,1,512]{4,3,2,1,0:T(1,128)} fusion(f32[2,5,256,3,512]{4,3,2,1,0:T(4,128)} %reshape.57), kind=kLoop, calls=%fused_computation.4 | loop fusion | flops 2621440 | bytes 31457280 | tf_op jit(solution)/shard_map/add | solution.py:132
  247.5 6.5 %fusion.2 = bf16[2,5,256,512]{3,2,1,0:T(8,128)(2,1)} fusion(f32[2,5,256,512]{3,2,1,0:T(8,128)} %bitcast.39, f32[2,5,256,1,512]{4,3,2,1,0:T(1,128)} %fusion.1), kind=kLoop, calls=%fused_computation.6 | loop fusion | flops 2621440 | bytes 13107200 | tf_op jit(solution)/shard_map/convert_element_type | solution.py:136
  (93 shorter events, 32.4 us)
Async XLA Ops:
  0.6 19.6 %copy-start = (bf16[512,18]{0,1:T(8,128)(2,1)S(1)}, bf16[512,18]{0,1:T(8,128)(2,1)}, u32[]{:S(2)}) copy-start(bf16[512,18]{0,1:T(8,128)(2,1)} %param.13) | copy-start | bytes 55300
  11.3 2.8 %copy-start.4 = (bf16[2,5,256,512]{3,2,1,0:T(8,128)(2,1)S(1)}, bf16[2,5,256,512]{3,2,1,0:T(8,128)(2,1)}, u32[]{:S(2)}) copy-start(bf16[2,5,256,512]{3,2,1,0:T(8,128)(2,1)} %param.9) | copy-start | bytes 7864324
  14.2 1.4 copy-start.6
  15.0 5.2 %copy-start.5 = (bf16[2,5,256,1536]{3,2,1,0:T(8,128)(2,1)}, bf16[2,5,256,1536]{3,2,1,0:T(8,128)(2,1)S(1)}, u32[]{:S(2)}) copy-start(bf16[2,5,256,1536]{3,2,1,0:T(8,128)(2,1)S(1)} %pad_maximum_fusion) | copy-start | bytes 23592964
  15.6 4.7 %copy-start.8 = (f32[512]{0:T(512)S(1)}, f32[512]{0:T(512)}, u32[]{:S(2)}) copy-start(f32[512]{0:T(512)} %param.12) | copy-start | bytes 6148
  15.6 4.7 %copy-start.9 = (f32[18]{0:T(128)S(1)}, f32[18]{0:T(128)}, u32[]{:S(2)}) copy-start(f32[18]{0:T(128)} %param.14) | copy-start | bytes 220
  20.2 2.3 copy-start.3
  20.3 2.3 copy-start.10
  79.8 6.4 %slice-start = ((s8[5242880]{0:T(1024)(128)(4,1)}), s8[4194304]{0:T(1024)(128)(4,1)S(1)}, s32[]{:S(2)}) async-start(s8[5242880]{0:T(1024)(128)(4,1)} %bitcast.40), calls=%async_computation.6 | async-start | bytes 8388608
  80.3 5.9 %slice-start.1 = ((s8[5242880]{0:T(1024)(128)(4,1)}), s8[1048576]{0:T(1024)(128)(4,1)S(1)}, s32[]{:S(2)}) async-start(s8[5242880]{0:T(1024)(128)(4,1)} %bitcast.40), calls=%async_computation.7 | async-start | bytes 2097152
  80.3 7.5 %slice-start.2 = ((s8[7864320]{0:T(1024)(128)(4,1)}), s8[4194304]{0:T(1024)(128)(4,1)S(1)}, s32[]{:S(2)}) async-start(s8[7864320]{0:T(1024)(128)(4,1)} %bitcast.45), calls=%async_computation.8 | async-start | bytes 8388608
  86.2 2.0 slice-start.3
  88.2 4.3 %copy-start.2 = (f32[2560,512]{1,0:T(8,128)}, f32[2560,512]{1,0:T(8,128)S(1)}, u32[]{:S(2)}) copy-start(f32[2560,512]{1,0:T(8,128)S(1)} %subtract_multiply_fusion) | copy-start | bytes 15728644
  160.6 8.1 %copy-start.7 = (bf16[1536,512]{1,0:T(8,128)(2,1)S(1)}, bf16[1536,512]{1,0:T(8,128)(2,1)}, u32[]{:S(2)}) copy-start(bf16[1536,512]{1,0:T(8,128)(2,1)} %param.11) | copy-start | bytes 4718596
  161.8 43.3 %all-to-all-start.3 = ((f32[64,6,512]{2,1,0:T(8,128)}), f32[64,6,512]{2,1,0:T(8,128)S(1)}, u32[]{:S(2)}, u32[]{:S(2)}) async-start(f32[64,6,512]{2,1,0:T(8,128)} %broadcast_in_dim.6), calls=%async_computation.3 | async-start | bytes 2097152 | tf_op jit(solution)/shard_map/all_to_all | solution.py:50
  220.6 33.4 %all-to-all-start.5 = ((bf16[2,768,512]{2,1,0:T(8,128)(2,1)}), bf16[2,768,512]{2,1,0:T(8,128)(2,1)S(1)}, u32[]{:S(2)}, u32[]{:S(2)}) async-start(bf16[2,768,512]{2,1,0:T(8,128)(2,1)} %broadcast_in_dim.8), calls=%async_computation.5 | async-start | bytes 3145728 | tf_op jit(solution)/shard_map/all_to_all | solution.py:50
  247.5 7.6 %copy-start.1 = (bf16[512,18]{0,1:T(8,128)(2,1)S(1)}, bf16[512,18]{0,1:T(8,128)(2,1)}, u32[]{:S(2)}) copy-start(bf16[512,18]{0,1:T(8,128)(2,1)} %param.13) | copy-start | bytes 55300
